TPU v7x, 32 devices: a whole 2x2x4 slice. The times are simulated.
32 devices in a mesh: ves: 4 (over x, core), shard: 8 (over z, y).
Axes of the slice: x: 2, y: 2, z: 4, core: 2. Of those that a mesh axis runs over, the one named last changes fastest.
Arguments:
- displacement: float32 [3, 8, 256, 128], P(None, 'ves', 'shard'), may hold values from -6 to 6
- tension: float32 [8], P('ves'), may hold values from 2 to 8
- bending: float32 [8], P('ves'), may hold values from 0.2 to 0.8
- offset: float32 [3, 8, 256, 128], P(None, 'ves', 'shard'), may hold values from 0 to 1
- owner: int32 [8, 256, 128], P('ves', 'shard'), may hold values from 0 to 31, as said below
- cell: int32 [8, 256, 128], P('ves', 'shard'), may hold values from 0 to 131071
- populations: float32 [64, 19, 256, 256], P(('ves', 'shard')), may hold values from 0 to 1, as said below
Outputs:
- membrane_force: float32 [3, 8, 256, 128], P(None, 'ves', 'shard')
- force_field: float32 [64, 3, 256, 256], P(('ves', 'shard'))
- new_populations: float32 [64, 19, 256, 256], P(('ves', 'shard'))
Inputs may be any that keep to these rules, and one draw needn't show every extreme that they name: The points of one device name any one owner at most 512 times, and some owner is named exactly 512 times by the points of every device. `populations`: entries are positive.
All inputs are finite; a program needn't handle non-finite values.
Results may differ from a plain program's by a relative error of at most 0.0061.
Values sent between devices are 32-bit elements; how exact they have to be, the bound alone decides.
A program may use at most 128 MiB of HBM per device.

v0:
```python
import math
import jax
import jax.numpy as jnp
from jax import lax
from jax.sharding import PartitionSpec as P

relax_time = 0.8
velocity_x = [0, 1, -1, 0, 0, 0, 1, -1, 0, 0, 0, 1, -1, 0, 0, 1, 1, -1, -1]
velocity_y = [0, 0, 0, 1, -1, 0, 0, 0, 1, -1, 0, 0, 0, 1, -1, 1, -1, 1, -1]
velocity_z = [1, 1, 1, 1, 1, -1, -1, -1, -1, -1, 0, 0, 0, 0, 0, 0, 0, 0, 0]
lattice_weights = [
    1.0 / 18,
    1.0 / 36,
    1.0 / 36,
    1.0 / 36,
    1.0 / 36,
    1.0 / 18,
    1.0 / 36,
    1.0 / 36,
    1.0 / 36,
    1.0 / 36,
    1.0 / 3,
    1.0 / 18,
    1.0 / 18,
    1.0 / 18,
    1.0 / 18,
    1.0 / 36,
    1.0 / 36,
    1.0 / 36,
    1.0 / 36,
]


def padded_2(x, sides, width):
    for axis, dim in sides:
        devices, length = (lax.axis_size(axis), x.shape[dim])
        up = [(i, (i + 1) % devices) for i in range(devices - 1)]
        down = [(j, i) for i, j in up]
        last = lax.slice_in_dim(x, length - width, length, axis=dim)
        initial = lax.slice_in_dim(x, 0, width, axis=dim)
        before = lax.ppermute(last, axis, up)
        after = lax.ppermute(initial, axis, down)
        x = jnp.concatenate([before, x, after], axis=dim)
    return x


def passed_along(value, axis, steps):
    count = lax.axis_size(axis)
    pairs = [(source, (source + steps) % count) for source in range(count)]
    return lax.ppermute(value, axis, pairs)


def kernel_weight(distance):
    return 0.25 * (1.0 + jnp.cos(0.5 * math.pi * distance))


def surface_laplacian(padded):
    center = padded[:, :, 1:-1]
    return (
        padded[:, :, 2:]
        + padded[:, :, :-2]
        + jnp.roll(center, 1, 3)
        + jnp.roll(center, -1, 3)
        - 4.0 * center
    )


def collide(populations, field):
    density = jnp.sum(populations, 1)
    moment_x = jnp.zeros_like(density)
    moment_y = jnp.zeros_like(density)
    moment_z = jnp.zeros_like(density)
    for item in range(19):
        moment_x = moment_x + velocity_x[item] * populations[:, item]
        moment_y = moment_y + velocity_y[item] * populations[:, item]
        moment_z = moment_z + velocity_z[item] * populations[:, item]
    flow_x = (moment_x + 0.5 * field[:, 0]) / density
    flow_y = (moment_y + 0.5 * field[:, 1]) / density
    flow_z = (moment_z + 0.5 * field[:, 2]) / density
    speed_sq = flow_x * flow_x + flow_y * flow_y + flow_z * flow_z
    result = []
    for item in range(19):
        ex, ey, ez = (velocity_x[item], velocity_y[item], velocity_z[item])
        weight = lattice_weights[item]
        along = ex * flow_x + ey * flow_y + ez * flow_z
        equilibrium = weight * density * (1.0 + 3.0 * along + 4.5 * along * along - 1.5 * speed_sq)
        push = (
            (ex - flow_x) * field[:, 0] + (ey - flow_y) * field[:, 1] + (ez - flow_z) * field[:, 2]
        )
        facing = ex * field[:, 0] + ey * field[:, 1] + ez * field[:, 2]
        source = weight * (3.0 * push + 9.0 * along * facing)
        current = populations[:, item]
        result.append(
            current - (current - equilibrium) / relax_time + (1.0 - 0.5 / relax_time) * source
        )
    return jnp.stack(result, 1)


def on_device(displacement, tension, bending, offset, owner, cell, populations):
    padded = padded_2(displacement, (("shard", 2),), 1)
    first = surface_laplacian(padded)
    padded_first = padded_2(first, (("shard", 2),), 1)
    second = surface_laplacian(padded_first)
    membrane_force = tension[None, :, None, None] * first - bending[None, :, None, None] * second
    ves_count = lax.axis_size("ves")
    shard_count = lax.axis_size("shard")
    device_count = ves_count * shard_count
    point_count = owner.size
    capacity = 2 * point_count // device_count
    slot_total = device_count * capacity
    payload = jnp.concatenate(
        [membrane_force.reshape(3, point_count), offset.reshape(3, point_count)], 0
    )
    owner_flat = owner.reshape(point_count)
    cell_flat = cell.reshape(point_count)
    order = jnp.argsort(owner_flat, stable=True)
    sorted_owner = owner_flat[order]
    matches = sorted_owner[:, None] == jnp.arange(device_count, dtype=jnp.int32)[None, :]
    counts = jnp.sum(matches.astype(jnp.int32), 0)
    starts = jnp.cumsum(counts) - counts
    first_place = jnp.sum(jnp.where(matches, starts[None, :], 0), 1)
    slot = sorted_owner * capacity + jnp.arange(point_count, dtype=jnp.int32) - first_place
    send_values = jnp.zeros((6, slot_total), jnp.float32).at[:, slot].set(payload[:, order])
    send_cells = jnp.zeros((1, slot_total), jnp.int32).at[0, slot].set(cell_flat[order])
    got_values, got_cells = (
        lax.all_to_all(
            send_values.reshape(6, device_count, capacity),
            ("ves", "shard"),
            split_axis=1,
            concat_axis=1,
            tiled=True,
        ),
        lax.all_to_all(
            send_cells.reshape(1, device_count, capacity),
            ("ves", "shard"),
            split_axis=1,
            concat_axis=1,
            tiled=True,
        ),
    )
    got_values = got_values.reshape(6, slot_total)
    got_cells = got_cells.reshape(slot_total)
    slab = populations.shape[0]
    width = populations.shape[2]
    depth = slab + 3
    block = min(1024, slot_total)
    turns = slot_total // block
    value_blocks = got_values.reshape(6, turns, block).transpose(1, 0, 2)
    cell_blocks = got_cells.reshape(turns, block)
    grid = jnp.arange(width, dtype=jnp.int32)
    layers = jnp.arange(depth, dtype=jnp.int32)

    def spread_block(total, items):
        values, cells = items
        plane = cells // (width * width)
        column_x = cells // width % width
        column_y = cells % width
        weight_x = jnp.zeros((block, width), jnp.float32)
        weight_y = jnp.zeros((block, width), jnp.float32)
        weight_z = jnp.zeros((block, depth), jnp.float32)
        for reach in range(-1, 3):
            weight_x = weight_x + jnp.where(
                grid[None, :] == ((column_x + reach) % width)[:, None],
                kernel_weight(values[3] - reach)[:, None],
                0.0,
            )
            weight_y = weight_y + jnp.where(
                grid[None, :] == ((column_y + reach) % width)[:, None],
                kernel_weight(values[4] - reach)[:, None],
                0.0,
            )
            weight_z = weight_z + jnp.where(
                layers[None, :] == (plane + reach + 1)[:, None],
                kernel_weight(values[5] - reach)[:, None],
                0.0,
            )
        scaled = values[0:3].T[:, None, :, None] * weight_z[:, :, None, None]
        left = (
            (scaled * weight_x[:, None, None, :])
            .astype(jnp.bfloat16)
            .reshape(block, depth * 3 * width)
        )
        right = weight_y.astype(jnp.bfloat16)
        product = lax.dot_general(
            left, right, (((0,), (0,)), ((), ())), preferred_element_type=jnp.float32
        )
        return (total + product, None)

    total, unused = lax.scan(
        spread_block,
        jnp.zeros((depth * 3 * width, width), jnp.float32),
        (value_blocks, cell_blocks),
    )
    spread = total.reshape(depth, 3, width, width)
    from_below = passed_along(spread[slab + 1 : slab + 3], ("ves", "shard"), 1)
    from_above = passed_along(spread[0:1], ("ves", "shard"), -1)
    force_field = spread[1 : slab + 1].at[0:2].add(from_below).at[slab - 1 : slab].add(from_above)
    post = collide(populations, force_field)
    low_part = passed_along(post[slab - 1, 0:5], ("ves", "shard"), 1)
    high_part = passed_along(post[0, 5:10], ("ves", "shard"), -1)
    low_source = jnp.concatenate([low_part[None], post[: slab - 1, 0:5]], 0)
    high_source = jnp.concatenate([post[1:, 5:10], high_part[None]], 0)
    source = jnp.concatenate([low_source, high_source, post[:, 10:]], 1)
    moved = [
        jnp.roll(source[:, item], (velocity_x[item], velocity_y[item]), (1, 2))
        for item in range(19)
    ]
    return (membrane_force, force_field, jnp.stack(moved, 1))


def solution(mesh):
    return jax.shard_map(
        on_device,
        mesh=mesh,
        in_specs=(
            P(None, "ves", "shard", None),
            P("ves"),
            P("ves"),
            P(None, "ves", "shard", None),
            P("ves", "shard", None),
            P("ves", "shard", None),
            P(("ves", "shard"), None, None, None),
        ),
        out_specs=(
            P(None, "ves", "shard", None),
            P(("ves", "shard"), None, None, None),
            P(("ves", "shard"), None, None, None),
        ),
        check_vma=False,
    )
```

profile of v0, /device:TPU:0, one launch (start us, length us, event | category | flops | bytes accessed | tf_op | source)
XLA Modules:
  0.0 650.7 jit_solution(11068581569204606611)
XLA Ops:
  1.4 4.9 collective-permute-start.1
  7.6 7.5 %sort.17 = (s32[8192]{0:T(1024)}, s32[8192]{0:T(1024)S(1)}) sort(s32[8192]{0:T(1024)} %bitcast.1380, s32[8192]{0:T(1024)S(1)} %iota.38), dimensions={0}, to_apply=%region_0.1 | sort | flops 106496 | bytes 131072 | tf_op jit(solution)/shard_map/jit(argsort)/sort | solution.py:116
  15.2 45.5 %gather_fusion = s32[8192]{0:T(1024)S(1)} fusion(s32[8192]{0:T(1024)S(1)} %bitcast.1381, s32[8192]{0:T(1024)S(1)} %fusion.372), kind=kCustom, calls=%fused_computation | custom fusion | bytes 98304 | tf_op jit(solution)/shard_map/gather | solution.py:117
  62.0 45.5 %gather_fusion.1 = s32[8192]{0:T(1024)S(1)} fusion(s32[8192]{0:T(1024)S(1)} %bitcast.1379, s32[8192]{0:T(1024)S(1)} %fusion.372), kind=kCustom, calls=%fused_computation.2 | custom fusion | bytes 98304 | tf_op jit(solution)/shard_map/gather | solution.py:124
  107.5 31.1 %scatter_custom_fusion.1 = s32[16384]{0:T(1024)} fusion(s32[8192]{0:T(1024)S(1)} %broadcast_select_fusion, s32[8192]{0:T(1024)S(1)} %gather_fusion.1, s32[]{:T(128)} %constant.337.clone.1), kind=kCustom, calls=%fused_computation.665 | custom fusion | bytes 65540
  138.6 7.0 %all-to-all-start.1 = ((s32[1,32,512]{2,0,1:T(1,128)}), s32[1,32,512]{2,0,1:T(1,128)S(1)}, u32[]{:S(2)}, u32[]{:S(2)}) async-start(s32[1,32,512]{2,0,1:T(1,128)} %bitcast.8), calls=%async_computation.1 | async-start | bytes 131072 | tf_op jit(solution)/shard_map/all_to_all | solution.py:133
  158.2 70.3 %scatter_custom_fusion = f32[6,16384]{0,1:T(8,128)} fusion(s32[8192]{0:T(1024)S(1)} %bitcast.1413, f32[6,8192]{0,1:T(8,128)} %copy.148, s32[8192]{0:T(1024)S(1)} %fusion.372, f32[]{:T(128)} %constant.338.clone.1), kind=kCustom, calls=%fused_computation.104 | custom fusion | bytes 393728 | tf_op jit(solution)/shard_map/scatter | solution.py:123
  228.5 6.0 copy.149
  234.5 6.0 all-to-all-start
  240.8 16.0 %all-to-all-done = f32[6,32,512]{2,0,1:T(8,128)S(1)} async-done(((f32[6,32,512]{2,0,1:T(8,128)}), f32[6,32,512]{2,0,1:T(8,128)S(1)}, u32[]{:S(2)}, u32[]{:S(2)}) %all-to-all-start) | async-done | bytes 393248 | tf_op jit(solution)/shard_map/all_to_all | solution.py:126
  257.2 253.5 %while.18 = (s32[]{:T(128)}, f32[3840,256]{1,0:T(8,128)}, f32[16,6,1024]{2,0,1:T(8,128)S(1)}, s32[16,1024]{1,0:T(8,128)S(1)}, s32[]{:T(128)}, /*index=5*/s32[]{:T(128)}, s32[]{}, s32[]{}, s32[]{}) while((s32[]{:T(128)}, f32[3840,256]{1,0:T(8,128)}, f32[16,6,1024]{2,0,1:T(8,128)S(1)}, s32[16,1024]{1,0:T(8,128)S(1)}, ...), condition=%wide.region_7.8_spmd.clone.clone, body=%wide.region_6.7_spmd.clone.clone.sunk | while | flops 2029383680 | bytes 26144940 | solution.py:189
  259.1 5.4 multiply_convert_fusion.2
  264.5 7.5 %convolution_add_fusion.2 = f32[3840,256]{1,0:T(8,128)} fusion(bf16[1024,3840]{0,1:T(8,128)(2,1)} %bitcast.1382, f32[3840,256]{1,0:T(8,128)} %get-tuple-element.434, pred[]{:T(512)S(6)} %compare.117, f32[1024]{0:T(1024)S(1)} %bitcast.1419, s32[1024]{0:T(1024)S(1)} %get-tuple-element.417, f32[1024]{0:T(1024)S(1)} %bitcast.1418, ...), kind=kOutput, calls=%fused_computation.8.clone.1 | convolution fusion | flops 2018377728 | bytes 15761409 | tf_op jit(solution)/shard_map/while/body/eval_jaxpr/dot_general | solution.py:184
  273.8 5.4 multiply_convert_fusion.2
  279.3 8.6 %convolution_add_fusion.2 = f32[3840,256]{1,0:T(8,128)} fusion(bf16[1024,3840]{0,1:T(8,128)(2,1)} %bitcast.1382, f32[3840,256]{1,0:T(8,128)} %get-tuple-element.434, pred[]{:T(512)S(6)} %compare.117, f32[1024]{0:T(1024)S(1)} %bitcast.1419, s32[1024]{0:T(1024)S(1)} %get-tuple-element.417, f32[1024]{0:T(1024)S(1)} %bitcast.1418, ...), kind=kOutput, calls=%fused_computation.8.clone.1 | convolution fusion | flops 2018377728 | bytes 15761409 | tf_op jit(solution)/shard_map/while/body/eval_jaxpr/dot_general | solution.py:184
  289.8 5.4 multiply_convert_fusion.2
  295.2 8.6 %convolution_add_fusion.2 = f32[3840,256]{1,0:T(8,128)} fusion(bf16[1024,3840]{0,1:T(8,128)(2,1)} %bitcast.1382, f32[3840,256]{1,0:T(8,128)} %get-tuple-element.434, pred[]{:T(512)S(6)} %compare.117, f32[1024]{0:T(1024)S(1)} %bitcast.1419, s32[1024]{0:T(1024)S(1)} %get-tuple-element.417, f32[1024]{0:T(1024)S(1)} %bitcast.1418, ...), kind=kOutput, calls=%fused_computation.8.clone.1 | convolution fusion | flops 2018377728 | bytes 15761409 | tf_op jit(solution)/shard_map/while/body/eval_jaxpr/dot_general | solution.py:184
  305.7 5.4 multiply_convert_fusion.2
  311.1 8.6 %convolution_add_fusion.2 = f32[3840,256]{1,0:T(8,128)} fusion(bf16[1024,3840]{0,1:T(8,128)(2,1)} %bitcast.1382, f32[3840,256]{1,0:T(8,128)} %get-tuple-element.434, pred[]{:T(512)S(6)} %compare.117, f32[1024]{0:T(1024)S(1)} %bitcast.1419, s32[1024]{0:T(1024)S(1)} %get-tuple-element.417, f32[1024]{0:T(1024)S(1)} %bitcast.1418, ...), kind=kOutput, calls=%fused_computation.8.clone.1 | convolution fusion | flops 2018377728 | bytes 15761409 | tf_op jit(solution)/shard_map/while/body/eval_jaxpr/dot_general | solution.py:184
  321.6 5.4 multiply_convert_fusion.2
  327.0 8.6 %convolution_add_fusion.2 = f32[3840,256]{1,0:T(8,128)} fusion(bf16[1024,3840]{0,1:T(8,128)(2,1)} %bitcast.1382, f32[3840,256]{1,0:T(8,128)} %get-tuple-element.434, pred[]{:T(512)S(6)} %compare.117, f32[1024]{0:T(1024)S(1)} %bitcast.1419, s32[1024]{0:T(1024)S(1)} %get-tuple-element.417, f32[1024]{0:T(1024)S(1)} %bitcast.1418, ...), kind=kOutput, calls=%fused_computation.8.clone.1 | convolution fusion | flops 2018377728 | bytes 15761409 | tf_op jit(solution)/shard_map/while/body/eval_jaxpr/dot_general | solution.py:184
  337.5 5.4 multiply_convert_fusion.2
  342.9 8.6 %convolution_add_fusion.2 = f32[3840,256]{1,0:T(8,128)} fusion(bf16[1024,3840]{0,1:T(8,128)(2,1)} %bitcast.1382, f32[3840,256]{1,0:T(8,128)} %get-tuple-element.434, pred[]{:T(512)S(6)} %compare.117, f32[1024]{0:T(1024)S(1)} %bitcast.1419, s32[1024]{0:T(1024)S(1)} %get-tuple-element.417, f32[1024]{0:T(1024)S(1)} %bitcast.1418, ...), kind=kOutput, calls=%fused_computation.8.clone.1 | convolution fusion | flops 2018377728 | bytes 15761409 | tf_op jit(solution)/shard_map/while/body/eval_jaxpr/dot_general | solution.py:184
  353.4 5.4 multiply_convert_fusion.2
  358.8 8.6 %convolution_add_fusion.2 = f32[3840,256]{1,0:T(8,128)} fusion(bf16[1024,3840]{0,1:T(8,128)(2,1)} %bitcast.1382, f32[3840,256]{1,0:T(8,128)} %get-tuple-element.434, pred[]{:T(512)S(6)} %compare.117, f32[1024]{0:T(1024)S(1)} %bitcast.1419, s32[1024]{0:T(1024)S(1)} %get-tuple-element.417, f32[1024]{0:T(1024)S(1)} %bitcast.1418, ...), kind=kOutput, calls=%fused_computation.8.clone.1 | convolution fusion | flops 2018377728 | bytes 15761409 | tf_op jit(solution)/shard_map/while/body/eval_jaxpr/dot_general | solution.py:184
  369.3 5.4 multiply_convert_fusion.2
  374.7 8.6 %convolution_add_fusion.2 = f32[3840,256]{1,0:T(8,128)} fusion(bf16[1024,3840]{0,1:T(8,128)(2,1)} %bitcast.1382, f32[3840,256]{1,0:T(8,128)} %get-tuple-element.434, pred[]{:T(512)S(6)} %compare.117, f32[1024]{0:T(1024)S(1)} %bitcast.1419, s32[1024]{0:T(1024)S(1)} %get-tuple-element.417, f32[1024]{0:T(1024)S(1)} %bitcast.1418, ...), kind=kOutput, calls=%fused_computation.8.clone.1 | convolution fusion | flops 2018377728 | bytes 15761409 | tf_op jit(solution)/shard_map/while/body/eval_jaxpr/dot_general | solution.py:184
  385.2 5.4 multiply_convert_fusion.2
  390.6 8.6 %convolution_add_fusion.2 = f32[3840,256]{1,0:T(8,128)} fusion(bf16[1024,3840]{0,1:T(8,128)(2,1)} %bitcast.1382, f32[3840,256]{1,0:T(8,128)} %get-tuple-element.434, pred[]{:T(512)S(6)} %compare.117, f32[1024]{0:T(1024)S(1)} %bitcast.1419, s32[1024]{0:T(1024)S(1)} %get-tuple-element.417, f32[1024]{0:T(1024)S(1)} %bitcast.1418, ...), kind=kOutput, calls=%fused_computation.8.clone.1 | convolution fusion | flops 2018377728 | bytes 15761409 | tf_op jit(solution)/shard_map/while/body/eval_jaxpr/dot_general | solution.py:184
  401.2 5.4 multiply_convert_fusion.2
  406.6 8.6 %convolution_add_fusion.2 = f32[3840,256]{1,0:T(8,128)} fusion(bf16[1024,3840]{0,1:T(8,128)(2,1)} %bitcast.1382, f32[3840,256]{1,0:T(8,128)} %get-tuple-element.434, pred[]{:T(512)S(6)} %compare.117, f32[1024]{0:T(1024)S(1)} %bitcast.1419, s32[1024]{0:T(1024)S(1)} %get-tuple-element.417, f32[1024]{0:T(1024)S(1)} %bitcast.1418, ...), kind=kOutput, calls=%fused_computation.8.clone.1 | convolution fusion | flops 2018377728 | bytes 15761409 | tf_op jit(solution)/shard_map/while/body/eval_jaxpr/dot_general | solution.py:184
  417.1 5.4 multiply_convert_fusion.2
  422.5 8.6 %convolution_add_fusion.2 = f32[3840,256]{1,0:T(8,128)} fusion(bf16[1024,3840]{0,1:T(8,128)(2,1)} %bitcast.1382, f32[3840,256]{1,0:T(8,128)} %get-tuple-element.434, pred[]{:T(512)S(6)} %compare.117, f32[1024]{0:T(1024)S(1)} %bitcast.1419, s32[1024]{0:T(1024)S(1)} %get-tuple-element.417, f32[1024]{0:T(1024)S(1)} %bitcast.1418, ...), kind=kOutput, calls=%fused_computation.8.clone.1 | convolution fusion | flops 2018377728 | bytes 15761409 | tf_op jit(solution)/shard_map/while/body/eval_jaxpr/dot_general | solution.py:184
  433.0 5.4 multiply_convert_fusion.2
  438.4 8.6 %convolution_add_fusion.2 = f32[3840,256]{1,0:T(8,128)} fusion(bf16[1024,3840]{0,1:T(8,128)(2,1)} %bitcast.1382, f32[3840,256]{1,0:T(8,128)} %get-tuple-element.434, pred[]{:T(512)S(6)} %compare.117, f32[1024]{0:T(1024)S(1)} %bitcast.1419, s32[1024]{0:T(1024)S(1)} %get-tuple-element.417, f32[1024]{0:T(1024)S(1)} %bitcast.1418, ...), kind=kOutput, calls=%fused_computation.8.clone.1 | convolution fusion | flops 2018377728 | bytes 15761409 | tf_op jit(solution)/shard_map/while/body/eval_jaxpr/dot_general | solution.py:184
  448.9 5.4 multiply_convert_fusion.2
  454.3 8.6 %convolution_add_fusion.2 = f32[3840,256]{1,0:T(8,128)} fusion(bf16[1024,3840]{0,1:T(8,128)(2,1)} %bitcast.1382, f32[3840,256]{1,0:T(8,128)} %get-tuple-element.434, pred[]{:T(512)S(6)} %compare.117, f32[1024]{0:T(1024)S(1)} %bitcast.1419, s32[1024]{0:T(1024)S(1)} %get-tuple-element.417, f32[1024]{0:T(1024)S(1)} %bitcast.1418, ...), kind=kOutput, calls=%fused_computation.8.clone.1 | convolution fusion | flops 2018377728 | bytes 15761409 | tf_op jit(solution)/shard_map/while/body/eval_jaxpr/dot_general | solution.py:184
  464.8 5.4 multiply_convert_fusion.2
  470.2 8.6 %convolution_add_fusion.2 = f32[3840,256]{1,0:T(8,128)} fusion(bf16[1024,3840]{0,1:T(8,128)(2,1)} %bitcast.1382, f32[3840,256]{1,0:T(8,128)} %get-tuple-element.434, pred[]{:T(512)S(6)} %compare.117, f32[1024]{0:T(1024)S(1)} %bitcast.1419, s32[1024]{0:T(1024)S(1)} %get-tuple-element.417, f32[1024]{0:T(1024)S(1)} %bitcast.1418, ...), kind=kOutput, calls=%fused_computation.8.clone.1 | convolution fusion | flops 2018377728 | bytes 15761409 | tf_op jit(solution)/shard_map/while/body/eval_jaxpr/dot_general | solution.py:184
  480.7 5.4 multiply_convert_fusion.2
  486.1 8.6 %convolution_add_fusion.2 = f32[3840,256]{1,0:T(8,128)} fusion(bf16[1024,3840]{0,1:T(8,128)(2,1)} %bitcast.1382, f32[3840,256]{1,0:T(8,128)} %get-tuple-element.434, pred[]{:T(512)S(6)} %compare.117, f32[1024]{0:T(1024)S(1)} %bitcast.1419, s32[1024]{0:T(1024)S(1)} %get-tuple-element.417, f32[1024]{0:T(1024)S(1)} %bitcast.1418, ...), kind=kOutput, calls=%fused_computation.8.clone.1 | convolution fusion | flops 2018377728 | bytes 15761409 | tf_op jit(solution)/shard_map/while/body/eval_jaxpr/dot_general | solution.py:184
  496.6 5.4 multiply_convert_fusion.2
  502.0 8.6 %convolution_add_fusion.2 = f32[3840,256]{1,0:T(8,128)} fusion(bf16[1024,3840]{0,1:T(8,128)(2,1)} %bitcast.1382, f32[3840,256]{1,0:T(8,128)} %get-tuple-element.434, pred[]{:T(512)S(6)} %compare.117, f32[1024]{0:T(1024)S(1)} %bitcast.1419, s32[1024]{0:T(1024)S(1)} %get-tuple-element.417, f32[1024]{0:T(1024)S(1)} %bitcast.1418, ...), kind=kOutput, calls=%fused_computation.8.clone.1 | convolution fusion | flops 2018377728 | bytes 15761409 | tf_op jit(solution)/shard_map/while/body/eval_jaxpr/dot_general | solution.py:184
  516.5 4.6 collective-permute-start.5
  521.2 4.7 reduce_sum.34
  525.9 40.6 %collective-permute-done.4 = f32[2,3,256,256]{3,2,1,0:T(8,128)} collective-permute-done((f32[2,3,256,256]{3,2,1,0:T(8,128)}, f32[2,3,256,256]{3,2,1,0:T(8,128)}, u32[]{:S(2)}, u32[]{:S(2)}) %collective-permute-start.4) | collective-permute-done | bytes 1572896 | tf_op jit(solution)/shard_map/ppermute | solution.py:50
  571.2 5.9 fusion.77
  592.4 50.1 %collective-permute-done.6 = f32[5,256,256]{2,1,0:T(8,128)S(1)} collective-permute-done((f32[5,256,256]{2,1,0:T(8,128)S(1)}, f32[5,256,256]{2,1,0:T(8,128)S(1)}, u32[]{:S(2)}, u32[]{:S(2)}) %collective-permute-start.6) | collective-permute-done | bytes 1310752 | tf_op jit(solution)/shard_map/ppermute | solution.py:50
  (280 shorter events, 78.6 us)
Async XLA Ops:
  0.6 61.3 %copy-start = (s32[2,32,128]{2,1,0:T(8,128)S(1)}, s32[2,32,128]{2,1,0:T(8,128)}, u32[]{:S(2)}) copy-start(s32[2,32,128]{2,1,0:T(8,128)} %param.20) | copy-start | bytes 98308
  0.6 14.5 %copy-start.2 = (s32[2,32,128]{2,1,0:T(8,128)S(1)}, s32[2,32,128]{2,1,0:T(8,128)}, u32[]{:S(2)}) copy-start(s32[2,32,128]{2,1,0:T(8,128)} %param.19) | copy-start | bytes 98308
  1.4 144.4 %collective-permute-start.1 = (f32[3,2,1,128]{3,2,1,0:T(1,128)S(1)}, f32[3,2,1,128]{3,2,1,0:T(1,128)S(1)}, u32[]{:S(2)}, u32[]{:S(2)}) collective-permute-start(f32[3,2,1,128]{3,2,1,0:T(1,128)S(1)} %get-tuple-element.346), channel_id=1, source_target_pairs={{0,1},{1,2},{2,3},{3,4},{4,5},{5,6},{6,7},{8,9},{9,10},{10,11},{11... | collective-permute-start | bytes 9224 | tf_op jit(solution)/shard_map/ppermute | solution.py:41
  6.3 139.5 %collective-permute-start = (f32[3,2,1,128]{3,2,1,0:T(1,128)S(1)}, f32[3,2,1,128]{3,2,1,0:T(1,128)S(1)}, u32[]{:S(2)}, u32[]{:S(2)}) collective-permute-start(f32[3,2,1,128]{3,2,1,0:T(1,128)S(1)} %get-tuple-element.345), channel_id=1, source_target_pairs={{1,0},{2,1},{3,2},{4,3},{5,4},{6,5},{7,6},{9,8},{10,9},{11,10},{12... | collective-permute-start | bytes 9224 | tf_op jit(solution)/shard_map/ppermute | solution.py:42
  15.2 46.4 %copy-start.11 = (s32[2]{0:T(128)S(1)}, s32[2]{0:T(128)}, u32[]{:S(2)}) copy-start(s32[2]{0:T(128)} %constant.369) | copy-start | bytes 28
  15.2 46.6 %copy-start.10 = (s32[2]{0:T(128)S(1)}, s32[2]{0:T(128)}, u32[]{:S(2)}) copy-start(s32[2]{0:T(128)} %constant.366) | copy-start | bytes 28
  61.9 83.6 %copy-start.4 = (f32[3,2,32,128]{3,2,1,0:T(8,128)S(1)}, f32[3,2,32,128]{3,2,1,0:T(8,128)}, u32[]{:S(2)}) copy-start(f32[3,2,32,128]{3,2,1,0:T(8,128)} %param.15) | copy-start | bytes 294916
  62.0 93.2 %copy-start.8 = (f32[2]{0:T(128)S(1)}, f32[2]{0:T(128)}, u32[]{:S(2)}) copy-start(f32[2]{0:T(128)} %param.17) | copy-start | bytes 28
  62.0 93.2 %copy-start.9 = (f32[2]{0:T(128)S(1)}, f32[2]{0:T(128)}, u32[]{:S(2)}) copy-start(f32[2]{0:T(128)} %param.16) | copy-start | bytes 28
  62.0 93.4 %copy-start.6 = (f32[3,2,32,128]{3,2,1,0:T(8,128)S(1)}, f32[3,2,32,128]{3,2,1,0:T(8,128)}, u32[]{:S(2)}) copy-start(f32[3,2,32,128]{3,2,1,0:T(8,128)} %param.18) | copy-start | bytes 294916
  138.6 95.9 %all-to-all-start.1 = ((s32[1,32,512]{2,0,1:T(1,128)}), s32[1,32,512]{2,0,1:T(1,128)S(1)}, u32[]{:S(2)}, u32[]{:S(2)}) async-start(s32[1,32,512]{2,0,1:T(1,128)} %bitcast.8), calls=%async_computation.1 | async-start | bytes 131072 | tf_op jit(solution)/shard_map/all_to_all | solution.py:133
  146.0 5.1 collective-permute-start.3
  149.7 5.5 collective-permute-start.2
  155.3 73.2 %copy-start.5 = (f32[3,2,32,128]{3,2,1,0:T(8,128)}, f32[3,2,32,128]{3,2,1,0:T(8,128)S(1)}, u32[]{:S(2)}) copy-start(f32[3,2,32,128]{3,2,1,0:T(8,128)S(1)} %fusion.366) | copy-start | bytes 294916
  234.5 22.3 %all-to-all-start = ((f32[6,32,512]{2,0,1:T(8,128)}), f32[6,32,512]{2,0,1:T(8,128)S(1)}, u32[]{:S(2)}, u32[]{:S(2)}) async-start(f32[6,32,512]{2,0,1:T(8,128)} %copy.149), calls=%async_computation | async-start | bytes 1048576 | tf_op jit(solution)/shard_map/all_to_all | solution.py:126
  514.4 52.0 %collective-permute-start.4 = (f32[2,3,256,256]{3,2,1,0:T(8,128)}, f32[2,3,256,256]{3,2,1,0:T(8,128)}, u32[]{:S(2)}, u32[]{:S(2)}) collective-permute-start(f32[2,3,256,256]{3,2,1,0:T(8,128)} %bitcast.10), channel_id=1, source_target_pairs={{0,1},{1,2},{2,3},{3,4},{4,5},{5,6},{6,7},{7,8},{8,9},{9,10},{10,1... | collective-permute-start | bytes 4718600 | tf_op jit(solution)/shard_map/ppermute | solution.py:50
  516.5 53.3 %collective-permute-start.5 = (f32[1,3,256,256]{3,2,1,0:T(8,128)S(1)}, f32[1,3,256,256]{3,2,1,0:T(8,128)}, u32[]{:S(2)}, u32[]{:S(2)}) collective-permute-start(f32[1,3,256,256]{3,2,1,0:T(8,128)S(1)} %bitcast.1401), channel_id=1, source_target_pairs={{0,31},{1,0},{2,1},{3,2},{4,3},{5,4},{6,5},{7,6},{8,7},{9,8},{10,9... | collective-permute-start | bytes 2359304 | tf_op jit(solution)/shard_map/ppermute | solution.py:50
  521.2 56.0 %slice-start = ((s8[9961472]{0:T(1024)(128)(4,1)}), s8[1572864]{0:T(1024)(128)(4,1)S(1)}, s32[]{:S(2)}) async-start(s8[9961472]{0:T(1024)(128)(4,1)} %bitcast.1383), calls=%async_computation.2 | async-start | bytes 3145728
  566.5 10.7 %slice-start.1 = ((s8[9961472]{0:T(1024)(128)(4,1)}), s8[4194304]{0:T(1024)(128)(4,1)S(1)}, s32[]{:S(2)}) async-start(s8[9961472]{0:T(1024)(128)(4,1)} %bitcast.1383), calls=%async_computation.3 | async-start | bytes 8388608
  571.2 73.5 %copy-start.3 = (f32[2,3,256,256]{3,2,1,0:T(8,128)}, f32[2,3,256,256]{3,2,1,0:T(8,128)S(1)}, u32[]{:S(2)}) copy-start(f32[2,3,256,256]{3,2,1,0:T(8,128)S(1)} %fusion.29) | copy-start | bytes 4718596
  571.2 6.0 slice-start.2
  584.6 59.0 %collective-permute-start.7 = (f32[5,256,256]{2,1,0:T(8,128)S(1)}, f32[5,256,256]{2,1,0:T(8,128)S(1)}, u32[]{:S(2)}, u32[]{:S(2)}) collective-permute-start(f32[5,256,256]{2,1,0:T(8,128)S(1)} %get-tuple-element.327), channel_id=1, source_target_pairs={{0,31},{1,0},{2,1},{3,2},{4,3},{5,4},{6,5},{7,6},{8,7},{9,8},{10,9... | collective-permute-start | bytes 3932168 | tf_op jit(solution)/shard_map/ppermute | solution.py:50
  585.8 56.7 %collective-permute-start.6 = (f32[5,256,256]{2,1,0:T(8,128)S(1)}, f32[5,256,256]{2,1,0:T(8,128)S(1)}, u32[]{:S(2)}, u32[]{:S(2)}) collective-permute-start(f32[5,256,256]{2,1,0:T(8,128)S(1)} %get-tuple-element.334), channel_id=1, source_target_pairs={{0,1},{1,2},{2,3},{3,4},{4,5},{5,6},{6,7},{7,8},{8,9},{9,10},{10,1... | collective-permute-start | bytes 3932168 | tf_op jit(solution)/shard_map/ppermute | solution.py:50
  645.5 5.0 copy-start.1
  646.5 3.9 copy-start.7
where the time goes:
time: 660 us; the launch traced here: 651 us
  local copies, waits for them, and re-layouts  214 us (32%)
  other arithmetic  153 us (23%)
  matrix products  137 us (21%)
  waiting for transfers between devices  112 us (17%)
  starting transfers between devices  32.1 us (5%)
    dot_general x16, matrix products, spread_block(): lax.dot_general(left, right, (((0,), (0,)), ((), ())), preferred_element_...  137 us
    ppermute x4, waiting for transfers between devices, passed_along(): return lax.ppermute(value, axis, pairs)  91.9 us
    convert_element_type x16, other arithmetic, spread_block(): left = (scaled * weight_x[:, None, None, :]).astype(jnp.bfloat16).reshape...  86.4 us
    scatter x1, local copies, waits for them, and re-layouts, on_device(): jnp.zeros((6, slot_total), jnp.float32).at[:, slot].set(payload[:, order])  70.3 us
    gather x1, local copies, waits for them, and re-layouts, on_device(): cell_flat[order]  45.5 us
    gather x1, local copies, waits for them, and re-layouts, on_device(): sorted_owner = owner_flat[order]  45.5 us
    unnamed x31, local copies, waits for them, and re-layouts  35.1 us
    mul x16, other arithmetic, kernel_weight(): return 0.25 * (1.0 + jnp.cos(0.5 * math.pi * distance))  20.8 us
  transfers between devices with their start and end apart: 10, of which 5 were waited for; matrix products, arithmetic and copies ran while one was open for 35% of the time, Pallas kernels for 0%

commit v1 on v0

--- a/solution.py
+++ b/solution.py
@@ -29,6 +29,18 @@
     1.0 / 36,
     1.0 / 36,
 ]
+
+
+def stacks_all_reach(arr_in, ax_name):
+    return jnp.concatenate(
+        lax.all_to_all(
+            jnp.stack(jnp.split(arr_in, lax.axis_size(ax_name), axis=1)),
+            ax_name,
+            split_axis=0,
+            concat_axis=0,
+        ),
+        axis=1,
+    )
 
 
 def padded_2(x, sides, width):
@@ -123,13 +135,7 @@
     send_values = jnp.zeros((6, slot_total), jnp.float32).at[:, slot].set(payload[:, order])
     send_cells = jnp.zeros((1, slot_total), jnp.int32).at[0, slot].set(cell_flat[order])
     got_values, got_cells = (
-        lax.all_to_all(
-            send_values.reshape(6, device_count, capacity),
-            ("ves", "shard"),
-            split_axis=1,
-            concat_axis=1,
-            tiled=True,
-        ),
+        stacks_all_reach(send_values.reshape(6, device_count, capacity), ("ves", "shard")),
         lax.all_to_all(
             send_cells.reshape(1, device_count, capacity),
             ("ves", "shard"),

time: 660 us -> 713 us (1.080)
  local copies, waits for them, and re-layouts: 214 us -> 270 us
    unnamed x31 -> x94, local copies, waits for them, and re-layouts: 35.1 us -> 88.5 us
    split x0 -> x2, local copies, waits for them, and re-layouts: none -> 7.38 us  [stacks_all_reach(): jnp.split(arr_in, lax.axis_size(ax_name), axis=1)]
  transfers between devices with their start and end apart: 10 -> 10, of which waited for: 5 -> 5; matrix products, arithmetic and copies ran while one was open for 35% -> 40% of each run, Pallas kernels for 0% -> 0%
where the time goes in v1:
time: 713 us; the launch traced here: 703 us
  local copies, waits for them, and re-layouts  270 us (38%)
  other arithmetic  154 us (22%)
  matrix products  137 us (19%)
  waiting for transfers between devices  108 us (15%)
  starting transfers between devices  31.6 us (4%)
    dot_general x16, matrix products, spread_block(): lax.dot_general(left, right, (((0,), (0,)), ((), ())), preferred_element_...  137 us
    ppermute x4, waiting for transfers between devices, passed_along(): return lax.ppermute(value, axis, pairs)  91.9 us
    unnamed x94, local copies, waits for them, and re-layouts  88.5 us
    convert_element_type x16, other arithmetic, spread_block(): left = (scaled * weight_x[:, None, None, :]).astype(jnp.bfloat16).reshape...  86.4 us
    scatter x1, local copies, waits for them, and re-layouts, on_device(): jnp.zeros((6, slot_total), jnp.float32).at[:, slot].set(payload[:, order])  70.9 us
    gather x1, local copies, waits for them, and re-layouts, on_device(): cell_flat[order]  45.5 us
    gather x1, local copies, waits for them, and re-layouts, on_device(): sorted_owner = owner_flat[order]  45.5 us
    mul x16, other arithmetic, kernel_weight(): return 0.25 * (1.0 + jnp.cos(0.5 * math.pi * distance))  20.8 us
  transfers between devices with their start and end apart: 10, of which 5 were waited for; matrix products, arithmetic and copies ran while one was open for 40% of the time, Pallas kernels for 0%

profile of v1, /device:TPU:0, one launch (start us, length us, event | category | flops | bytes accessed | tf_op | source)
XLA Modules:
  0.0 703.4 jit_solution(13962440777952094728)
XLA Ops:
  1.4 4.9 collective-permute-start.1
  7.6 7.5 %sort.17 = (s32[8192]{0:T(1024)}, s32[8192]{0:T(1024)S(1)}) sort(s32[8192]{0:T(1024)} %bitcast.1449, s32[8192]{0:T(1024)S(1)} %iota.38), dimensions={0}, to_apply=%region_0.1 | sort | flops 106496 | bytes 131072 | tf_op jit(solution)/shard_map/jit(argsort)/sort | solution.py:128
  15.2 45.5 %gather_fusion = s32[8192]{0:T(1024)S(1)} fusion(s32[8192]{0:T(1024)S(1)} %bitcast.1450, s32[8192]{0:T(1024)S(1)} %fusion.372), kind=kCustom, calls=%fused_computation | custom fusion | bytes 98304 | tf_op jit(solution)/shard_map/gather | solution.py:129
  62.0 45.5 %gather_fusion.1 = s32[8192]{0:T(1024)S(1)} fusion(s32[8192]{0:T(1024)S(1)} %bitcast.1448, s32[8192]{0:T(1024)S(1)} %fusion.372), kind=kCustom, calls=%fused_computation.2 | custom fusion | bytes 98304 | tf_op jit(solution)/shard_map/gather | solution.py:136
  107.5 31.1 %scatter_custom_fusion.1 = s32[16384]{0:T(1024)} fusion(s32[8192]{0:T(1024)S(1)} %broadcast_select_fusion, s32[8192]{0:T(1024)S(1)} %gather_fusion.1, s32[]{:T(128)} %constant.337.clone.1), kind=kCustom, calls=%fused_computation.697 | custom fusion | bytes 65540
  138.6 7.1 %all-to-all-start.1 = ((s32[1,32,512]{2,0,1:T(1,128)}), s32[1,32,512]{2,0,1:T(1,128)}, u32[]{:S(2)}, u32[]{:S(2)}) async-start(s32[1,32,512]{2,0,1:T(1,128)} %bitcast.41), calls=%async_computation.1 | async-start | bytes 131072 | tf_op jit(solution)/shard_map/all_to_all | solution.py:139
  151.2 4.1 collective-permute-done.2
  158.3 70.9 %scatter_custom_fusion = f32[6,16384]{0,1:T(8,128)} fusion(s32[8192]{0:T(1024)S(1)} %bitcast.1484, f32[6,8192]{0,1:T(8,128)} %copy.287, s32[8192]{0:T(1024)S(1)} %fusion.372, f32[]{:T(128)} %constant.338.clone.1), kind=kCustom, calls=%fused_computation.104 | custom fusion | bytes 393728 | tf_op jit(solution)/shard_map/scatter | solution.py:135
  290.6 5.5 all-to-all-start
  297.2 12.4 %all-to-all-done = f32[32,6,1,512]{3,2,1,0:T(1,128)S(1)} async-done(((f32[32,6,1,512]{3,2,1,0:T(1,128)}), f32[32,6,1,512]{3,2,1,0:T(1,128)S(1)}, u32[]{:S(2)}, u32[]{:S(2)}) %all-to-all-start) | async-done | bytes 393248 | tf_op jit(solution)/shard_map/all_to_all | solution.py:36
  309.8 253.6 %while.18 = (s32[]{:T(128)}, f32[3840,256]{1,0:T(8,128)}, f32[16,6,1024]{2,0,1:T(8,128)S(1)}, s32[16,1024]{1,0:T(8,128)S(1)}, s32[]{:T(128)}, /*index=5*/s32[]{:T(128)}, s32[]{}, s32[]{}, s32[]{}) while((s32[]{:T(128)}, f32[3840,256]{1,0:T(8,128)}, f32[16,6,1024]{2,0,1:T(8,128)S(1)}, s32[16,1024]{1,0:T(8,128)S(1)}, ...), condition=%wide.region_7.8_spmd.clone.clone, body=%wide.region_6.7_spmd.clone.clone.sunk | while | flops 2029383680 | bytes 26144940 | solution.py:195
  311.7 5.4 multiply_convert_fusion.2
  317.1 7.5 %convolution_add_fusion.2 = f32[3840,256]{1,0:T(8,128)} fusion(bf16[1024,3840]{0,1:T(8,128)(2,1)} %bitcast.1451, f32[3840,256]{1,0:T(8,128)} %get-tuple-element.470, pred[]{:T(512)S(6)} %compare.117, f32[1024]{0:T(1024)S(1)} %bitcast.1490, s32[1024]{0:T(1024)S(1)} %get-tuple-element.453, f32[1024]{0:T(1024)S(1)} %bitcast.1489, ...), kind=kOutput, calls=%fused_computation.8.clone.1 | convolution fusion | flops 2018377728 | bytes 15761409 | tf_op jit(solution)/shard_map/while/body/eval_jaxpr/dot_general | solution.py:190
  326.5 5.4 multiply_convert_fusion.2
  331.9 8.6 %convolution_add_fusion.2 = f32[3840,256]{1,0:T(8,128)} fusion(bf16[1024,3840]{0,1:T(8,128)(2,1)} %bitcast.1451, f32[3840,256]{1,0:T(8,128)} %get-tuple-element.470, pred[]{:T(512)S(6)} %compare.117, f32[1024]{0:T(1024)S(1)} %bitcast.1490, s32[1024]{0:T(1024)S(1)} %get-tuple-element.453, f32[1024]{0:T(1024)S(1)} %bitcast.1489, ...), kind=kOutput, calls=%fused_computation.8.clone.1 | convolution fusion | flops 2018377728 | bytes 15761409 | tf_op jit(solution)/shard_map/while/body/eval_jaxpr/dot_general | solution.py:190
  342.4 5.4 multiply_convert_fusion.2
  347.8 8.6 %convolution_add_fusion.2 = f32[3840,256]{1,0:T(8,128)} fusion(bf16[1024,3840]{0,1:T(8,128)(2,1)} %bitcast.1451, f32[3840,256]{1,0:T(8,128)} %get-tuple-element.470, pred[]{:T(512)S(6)} %compare.117, f32[1024]{0:T(1024)S(1)} %bitcast.1490, s32[1024]{0:T(1024)S(1)} %get-tuple-element.453, f32[1024]{0:T(1024)S(1)} %bitcast.1489, ...), kind=kOutput, calls=%fused_computation.8.clone.1 | convolution fusion | flops 2018377728 | bytes 15761409 | tf_op jit(solution)/shard_map/while/body/eval_jaxpr/dot_general | solution.py:190
  358.3 5.4 multiply_convert_fusion.2
  363.7 8.6 %convolution_add_fusion.2 = f32[3840,256]{1,0:T(8,128)} fusion(bf16[1024,3840]{0,1:T(8,128)(2,1)} %bitcast.1451, f32[3840,256]{1,0:T(8,128)} %get-tuple-element.470, pred[]{:T(512)S(6)} %compare.117, f32[1024]{0:T(1024)S(1)} %bitcast.1490, s32[1024]{0:T(1024)S(1)} %get-tuple-element.453, f32[1024]{0:T(1024)S(1)} %bitcast.1489, ...), kind=kOutput, calls=%fused_computation.8.clone.1 | convolution fusion | flops 2018377728 | bytes 15761409 | tf_op jit(solution)/shard_map/while/body/eval_jaxpr/dot_general | solution.py:190
  374.2 5.4 multiply_convert_fusion.2
  379.6 8.6 %convolution_add_fusion.2 = f32[3840,256]{1,0:T(8,128)} fusion(bf16[1024,3840]{0,1:T(8,128)(2,1)} %bitcast.1451, f32[3840,256]{1,0:T(8,128)} %get-tuple-element.470, pred[]{:T(512)S(6)} %compare.117, f32[1024]{0:T(1024)S(1)} %bitcast.1490, s32[1024]{0:T(1024)S(1)} %get-tuple-element.453, f32[1024]{0:T(1024)S(1)} %bitcast.1489, ...), kind=kOutput, calls=%fused_computation.8.clone.1 | convolution fusion | flops 2018377728 | bytes 15761409 | tf_op jit(solution)/shard_map/while/body/eval_jaxpr/dot_general | solution.py:190
  390.1 5.4 multiply_convert_fusion.2
  395.5 8.6 %convolution_add_fusion.2 = f32[3840,256]{1,0:T(8,128)} fusion(bf16[1024,3840]{0,1:T(8,128)(2,1)} %bitcast.1451, f32[3840,256]{1,0:T(8,128)} %get-tuple-element.470, pred[]{:T(512)S(6)} %compare.117, f32[1024]{0:T(1024)S(1)} %bitcast.1490, s32[1024]{0:T(1024)S(1)} %get-tuple-element.453, f32[1024]{0:T(1024)S(1)} %bitcast.1489, ...), kind=kOutput, calls=%fused_computation.8.clone.1 | convolution fusion | flops 2018377728 | bytes 15761409 | tf_op jit(solution)/shard_map/while/body/eval_jaxpr/dot_general | solution.py:190
  406.0 5.4 multiply_convert_fusion.2
  411.4 8.6 %convolution_add_fusion.2 = f32[3840,256]{1,0:T(8,128)} fusion(bf16[1024,3840]{0,1:T(8,128)(2,1)} %bitcast.1451, f32[3840,256]{1,0:T(8,128)} %get-tuple-element.470, pred[]{:T(512)S(6)} %compare.117, f32[1024]{0:T(1024)S(1)} %bitcast.1490, s32[1024]{0:T(1024)S(1)} %get-tuple-element.453, f32[1024]{0:T(1024)S(1)} %bitcast.1489, ...), kind=kOutput, calls=%fused_computation.8.clone.1 | convolution fusion | flops 2018377728 | bytes 15761409 | tf_op jit(solution)/shard_map/while/body/eval_jaxpr/dot_general | solution.py:190
  422.0 5.4 multiply_convert_fusion.2
  427.4 8.6 %convolution_add_fusion.2 = f32[3840,256]{1,0:T(8,128)} fusion(bf16[1024,3840]{0,1:T(8,128)(2,1)} %bitcast.1451, f32[3840,256]{1,0:T(8,128)} %get-tuple-element.470, pred[]{:T(512)S(6)} %compare.117, f32[1024]{0:T(1024)S(1)} %bitcast.1490, s32[1024]{0:T(1024)S(1)} %get-tuple-element.453, f32[1024]{0:T(1024)S(1)} %bitcast.1489, ...), kind=kOutput, calls=%fused_computation.8.clone.1 | convolution fusion | flops 2018377728 | bytes 15761409 | tf_op jit(solution)/shard_map/while/body/eval_jaxpr/dot_general | solution.py:190
  437.9 5.4 multiply_convert_fusion.2
  443.3 8.6 %convolution_add_fusion.2 = f32[3840,256]{1,0:T(8,128)} fusion(bf16[1024,3840]{0,1:T(8,128)(2,1)} %bitcast.1451, f32[3840,256]{1,0:T(8,128)} %get-tuple-element.470, pred[]{:T(512)S(6)} %compare.117, f32[1024]{0:T(1024)S(1)} %bitcast.1490, s32[1024]{0:T(1024)S(1)} %get-tuple-element.453, f32[1024]{0:T(1024)S(1)} %bitcast.1489, ...), kind=kOutput, calls=%fused_computation.8.clone.1 | convolution fusion | flops 2018377728 | bytes 15761409 | tf_op jit(solution)/shard_map/while/body/eval_jaxpr/dot_general | solution.py:190
  453.8 5.4 multiply_convert_fusion.2
  459.2 8.6 %convolution_add_fusion.2 = f32[3840,256]{1,0:T(8,128)} fusion(bf16[1024,3840]{0,1:T(8,128)(2,1)} %bitcast.1451, f32[3840,256]{1,0:T(8,128)} %get-tuple-element.470, pred[]{:T(512)S(6)} %compare.117, f32[1024]{0:T(1024)S(1)} %bitcast.1490, s32[1024]{0:T(1024)S(1)} %get-tuple-element.453, f32[1024]{0:T(1024)S(1)} %bitcast.1489, ...), kind=kOutput, calls=%fused_computation.8.clone.1 | convolution fusion | flops 2018377728 | bytes 15761409 | tf_op jit(solution)/shard_map/while/body/eval_jaxpr/dot_general | solution.py:190
  469.7 5.4 multiply_convert_fusion.2
  475.1 8.6 %convolution_add_fusion.2 = f32[3840,256]{1,0:T(8,128)} fusion(bf16[1024,3840]{0,1:T(8,128)(2,1)} %bitcast.1451, f32[3840,256]{1,0:T(8,128)} %get-tuple-element.470, pred[]{:T(512)S(6)} %compare.117, f32[1024]{0:T(1024)S(1)} %bitcast.1490, s32[1024]{0:T(1024)S(1)} %get-tuple-element.453, f32[1024]{0:T(1024)S(1)} %bitcast.1489, ...), kind=kOutput, calls=%fused_computation.8.clone.1 | convolution fusion | flops 2018377728 | bytes 15761409 | tf_op jit(solution)/shard_map/while/body/eval_jaxpr/dot_general | solution.py:190
  485.6 5.4 multiply_convert_fusion.2
  491.0 8.6 %convolution_add_fusion.2 = f32[3840,256]{1,0:T(8,128)} fusion(bf16[1024,3840]{0,1:T(8,128)(2,1)} %bitcast.1451, f32[3840,256]{1,0:T(8,128)} %get-tuple-element.470, pred[]{:T(512)S(6)} %compare.117, f32[1024]{0:T(1024)S(1)} %bitcast.1490, s32[1024]{0:T(1024)S(1)} %get-tuple-element.453, f32[1024]{0:T(1024)S(1)} %bitcast.1489, ...), kind=kOutput, calls=%fused_computation.8.clone.1 | convolution fusion | flops 2018377728 | bytes 15761409 | tf_op jit(solution)/shard_map/while/body/eval_jaxpr/dot_general | solution.py:190
  501.5 5.4 multiply_convert_fusion.2
  506.9 8.6 %convolution_add_fusion.2 = f32[3840,256]{1,0:T(8,128)} fusion(bf16[1024,3840]{0,1:T(8,128)(2,1)} %bitcast.1451, f32[3840,256]{1,0:T(8,128)} %get-tuple-element.470, pred[]{:T(512)S(6)} %compare.117, f32[1024]{0:T(1024)S(1)} %bitcast.1490, s32[1024]{0:T(1024)S(1)} %get-tuple-element.453, f32[1024]{0:T(1024)S(1)} %bitcast.1489, ...), kind=kOutput, calls=%fused_computation.8.clone.1 | convolution fusion | flops 2018377728 | bytes 15761409 | tf_op jit(solution)/shard_map/while/body/eval_jaxpr/dot_general | solution.py:190
  517.4 5.4 multiply_convert_fusion.2
  522.8 8.6 %convolution_add_fusion.2 = f32[3840,256]{1,0:T(8,128)} fusion(bf16[1024,3840]{0,1:T(8,128)(2,1)} %bitcast.1451, f32[3840,256]{1,0:T(8,128)} %get-tuple-element.470, pred[]{:T(512)S(6)} %compare.117, f32[1024]{0:T(1024)S(1)} %bitcast.1490, s32[1024]{0:T(1024)S(1)} %get-tuple-element.453, f32[1024]{0:T(1024)S(1)} %bitcast.1489, ...), kind=kOutput, calls=%fused_computation.8.clone.1 | convolution fusion | flops 2018377728 | bytes 15761409 | tf_op jit(solution)/shard_map/while/body/eval_jaxpr/dot_general | solution.py:190
  533.4 5.4 multiply_convert_fusion.2
  538.8 8.6 %convolution_add_fusion.2 = f32[3840,256]{1,0:T(8,128)} fusion(bf16[1024,3840]{0,1:T(8,128)(2,1)} %bitcast.1451, f32[3840,256]{1,0:T(8,128)} %get-tuple-element.470, pred[]{:T(512)S(6)} %compare.117, f32[1024]{0:T(1024)S(1)} %bitcast.1490, s32[1024]{0:T(1024)S(1)} %get-tuple-element.453, f32[1024]{0:T(1024)S(1)} %bitcast.1489, ...), kind=kOutput, calls=%fused_computation.8.clone.1 | convolution fusion | flops 2018377728 | bytes 15761409 | tf_op jit(solution)/shard_map/while/body/eval_jaxpr/dot_general | solution.py:190
  549.3 5.4 multiply_convert_fusion.2
  554.7 8.6 %convolution_add_fusion.2 = f32[3840,256]{1,0:T(8,128)} fusion(bf16[1024,3840]{0,1:T(8,128)(2,1)} %bitcast.1451, f32[3840,256]{1,0:T(8,128)} %get-tuple-element.470, pred[]{:T(512)S(6)} %compare.117, f32[1024]{0:T(1024)S(1)} %bitcast.1490, s32[1024]{0:T(1024)S(1)} %get-tuple-element.453, f32[1024]{0:T(1024)S(1)} %bitcast.1489, ...), kind=kOutput, calls=%fused_computation.8.clone.1 | convolution fusion | flops 2018377728 | bytes 15761409 | tf_op jit(solution)/shard_map/while/body/eval_jaxpr/dot_general | solution.py:190
  569.2 4.6 collective-permute-start.5
  573.8 4.7 reduce_sum.34
  578.5 40.7 %collective-permute-done.4 = f32[2,3,256,256]{3,2,1,0:T(8,128)} collective-permute-done((f32[2,3,256,256]{3,2,1,0:T(8,128)}, f32[2,3,256,256]{3,2,1,0:T(8,128)}, u32[]{:S(2)}, u32[]{:S(2)}) %collective-permute-start.4) | collective-permute-done | bytes 1572896 | tf_op jit(solution)/shard_map/ppermute | solution.py:62
  623.9 5.9 fusion.77
  645.1 50.1 %collective-permute-done.6 = f32[5,256,256]{2,1,0:T(8,128)S(1)} collective-permute-done((f32[5,256,256]{2,1,0:T(8,128)S(1)}, f32[5,256,256]{2,1,0:T(8,128)S(1)}, u32[]{:S(2)}, u32[]{:S(2)}) %collective-permute-start.6) | collective-permute-done | bytes 1310752 | tf_op jit(solution)/shard_map/ppermute | solution.py:62
  (345 shorter events, 136.6 us)
Async XLA Ops:
  0.6 61.3 %copy-start = (s32[2,32,128]{2,1,0:T(8,128)S(1)}, s32[2,32,128]{2,1,0:T(8,128)}, u32[]{:S(2)}) copy-start(s32[2,32,128]{2,1,0:T(8,128)} %param.20) | copy-start | bytes 98308
  0.6 14.5 %copy-start.2 = (s32[2,32,128]{2,1,0:T(8,128)S(1)}, s32[2,32,128]{2,1,0:T(8,128)}, u32[]{:S(2)}) copy-start(s32[2,32,128]{2,1,0:T(8,128)} %param.19) | copy-start | bytes 98308
  1.4 144.5 %collective-permute-start.1 = (f32[3,2,1,128]{3,2,1,0:T(1,128)S(1)}, f32[3,2,1,128]{3,2,1,0:T(1,128)S(1)}, u32[]{:S(2)}, u32[]{:S(2)}) collective-permute-start(f32[3,2,1,128]{3,2,1,0:T(1,128)S(1)} %get-tuple-element.382), channel_id=1, source_target_pairs={{0,1},{1,2},{2,3},{3,4},{4,5},{5,6},{6,7},{8,9},{9,10},{10,11},{11... | collective-permute-start | bytes 9224 | tf_op jit(solution)/shard_map/ppermute | solution.py:53
  6.3 139.6 %collective-permute-start = (f32[3,2,1,128]{3,2,1,0:T(1,128)S(1)}, f32[3,2,1,128]{3,2,1,0:T(1,128)S(1)}, u32[]{:S(2)}, u32[]{:S(2)}) collective-permute-start(f32[3,2,1,128]{3,2,1,0:T(1,128)S(1)} %get-tuple-element.381), channel_id=1, source_target_pairs={{1,0},{2,1},{3,2},{4,3},{5,4},{6,5},{7,6},{9,8},{10,9},{11,10},{12... | collective-permute-start | bytes 9224 | tf_op jit(solution)/shard_map/ppermute | solution.py:54
  15.2 46.4 %copy-start.11 = (s32[2]{0:T(128)S(1)}, s32[2]{0:T(128)}, u32[]{:S(2)}) copy-start(s32[2]{0:T(128)} %constant.369) | copy-start | bytes 28
  15.2 46.6 %copy-start.10 = (s32[2]{0:T(128)S(1)}, s32[2]{0:T(128)}, u32[]{:S(2)}) copy-start(s32[2]{0:T(128)} %constant.366) | copy-start | bytes 28
  61.9 83.8 %copy-start.4 = (f32[3,2,32,128]{3,2,1,0:T(8,128)S(1)}, f32[3,2,32,128]{3,2,1,0:T(8,128)}, u32[]{:S(2)}) copy-start(f32[3,2,32,128]{3,2,1,0:T(8,128)} %param.15) | copy-start | bytes 294916
  62.0 93.3 %copy-start.8 = (f32[2]{0:T(128)S(1)}, f32[2]{0:T(128)}, u32[]{:S(2)}) copy-start(f32[2]{0:T(128)} %param.17) | copy-start | bytes 28
  62.0 93.3 %copy-start.9 = (f32[2]{0:T(128)S(1)}, f32[2]{0:T(128)}, u32[]{:S(2)}) copy-start(f32[2]{0:T(128)} %param.16) | copy-start | bytes 28
  62.0 93.4 %copy-start.6 = (f32[3,2,32,128]{3,2,1,0:T(8,128)S(1)}, f32[3,2,32,128]{3,2,1,0:T(8,128)}, u32[]{:S(2)}) copy-start(f32[3,2,32,128]{3,2,1,0:T(8,128)} %param.18) | copy-start | bytes 294916
  138.6 152.0 %all-to-all-start.1 = ((s32[1,32,512]{2,0,1:T(1,128)}), s32[1,32,512]{2,0,1:T(1,128)}, u32[]{:S(2)}, u32[]{:S(2)}) async-start(s32[1,32,512]{2,0,1:T(1,128)} %bitcast.41), calls=%async_computation.1 | async-start | bytes 131072 | tf_op jit(solution)/shard_map/all_to_all | solution.py:139
  146.2 5.0 collective-permute-start.3
  149.8 5.5 collective-permute-start.2
  155.4 73.7 %copy-start.5 = (f32[3,2,32,128]{3,2,1,0:T(8,128)}, f32[3,2,32,128]{3,2,1,0:T(8,128)S(1)}, u32[]{:S(2)}) copy-start(f32[3,2,32,128]{3,2,1,0:T(8,128)S(1)} %fusion.366) | copy-start | bytes 294916
  290.6 18.9 %all-to-all-start = ((f32[32,6,1,512]{3,2,1,0:T(1,128)}), f32[32,6,1,512]{3,2,1,0:T(1,128)S(1)}, u32[]{:S(2)}, u32[]{:S(2)}) async-start(f32[32,6,1,512]{3,2,1,0:T(1,128)} %constant_dynamic-update-slice_fusion), calls=%async_computation | async-start | bytes 786432 | tf_op jit(solution)/shard_map/all_to_all | solution.py:36
  567.1 52.1 %collective-permute-start.4 = (f32[2,3,256,256]{3,2,1,0:T(8,128)}, f32[2,3,256,256]{3,2,1,0:T(8,128)}, u32[]{:S(2)}, u32[]{:S(2)}) collective-permute-start(f32[2,3,256,256]{3,2,1,0:T(8,128)} %bitcast.43), channel_id=1, source_target_pairs={{0,1},{1,2},{2,3},{3,4},{4,5},{5,6},{6,7},{7,8},{8,9},{9,10},{10,1... | collective-permute-start | bytes 4718600 | tf_op jit(solution)/shard_map/ppermute | solution.py:62
  569.2 53.3 %collective-permute-start.5 = (f32[1,3,256,256]{3,2,1,0:T(8,128)S(1)}, f32[1,3,256,256]{3,2,1,0:T(8,128)}, u32[]{:S(2)}, u32[]{:S(2)}) collective-permute-start(f32[1,3,256,256]{3,2,1,0:T(8,128)S(1)} %bitcast.1472), channel_id=1, source_target_pairs={{0,31},{1,0},{2,1},{3,2},{4,3},{5,4},{6,5},{7,6},{8,7},{9,8},{10,9... | collective-permute-start | bytes 2359304 | tf_op jit(solution)/shard_map/ppermute | solution.py:62
  573.8 56.0 %slice-start = ((s8[9961472]{0:T(1024)(128)(4,1)}), s8[1572864]{0:T(1024)(128)(4,1)S(1)}, s32[]{:S(2)}) async-start(s8[9961472]{0:T(1024)(128)(4,1)} %bitcast.1452), calls=%async_computation.2 | async-start | bytes 3145728
  619.1 10.7 %slice-start.1 = ((s8[9961472]{0:T(1024)(128)(4,1)}), s8[4194304]{0:T(1024)(128)(4,1)S(1)}, s32[]{:S(2)}) async-start(s8[9961472]{0:T(1024)(128)(4,1)} %bitcast.1452), calls=%async_computation.3 | async-start | bytes 8388608
  623.9 73.5 %copy-start.3 = (f32[2,3,256,256]{3,2,1,0:T(8,128)}, f32[2,3,256,256]{3,2,1,0:T(8,128)S(1)}, u32[]{:S(2)}) copy-start(f32[2,3,256,256]{3,2,1,0:T(8,128)S(1)} %fusion.29) | copy-start | bytes 4718596
  623.9 6.0 slice-start.2
  637.3 59.0 %collective-permute-start.7 = (f32[5,256,256]{2,1,0:T(8,128)S(1)}, f32[5,256,256]{2,1,0:T(8,128)S(1)}, u32[]{:S(2)}, u32[]{:S(2)}) collective-permute-start(f32[5,256,256]{2,1,0:T(8,128)S(1)} %get-tuple-element.363), channel_id=1, source_target_pairs={{0,31},{1,0},{2,1},{3,2},{4,3},{5,4},{6,5},{7,6},{8,7},{9,8},{10,9... | collective-permute-start | bytes 3932168 | tf_op jit(solution)/shard_map/ppermute | solution.py:62
  638.4 56.8 %collective-permute-start.6 = (f32[5,256,256]{2,1,0:T(8,128)S(1)}, f32[5,256,256]{2,1,0:T(8,128)S(1)}, u32[]{:S(2)}, u32[]{:S(2)}) collective-permute-start(f32[5,256,256]{2,1,0:T(8,128)S(1)} %get-tuple-element.370), channel_id=1, source_target_pairs={{0,1},{1,2},{2,3},{3,4},{4,5},{5,6},{6,7},{7,8},{8,9},{9,10},{10,1... | collective-permute-start | bytes 3932168 | tf_op jit(solution)/shard_map/ppermute | solution.py:62
  698.1 5.0 copy-start.1
  699.2 3.9 copy-start.7
